TPU v7x, 32 devices: a whole 2x2x4 slice. The times are simulated.
32 devices in a mesh: space: 4 (over y, x), exc: 8 (over z, core).
Axes of the slice: x: 2, y: 2, z: 4, core: 2. Of those that a mesh axis runs over, the one named last changes fastest.
Arguments:
- coeff: float32 [64, 256, 4096], P('space', None, 'exc'), may hold values from -6 to 6
- factors: float32 [4, 64, 256, 512], P(None, 'space', 'exc'), may hold values from -0.25 to 0.25
Outputs:
- applied: float32 [64, 256, 4096], P('space', None, 'exc')
All inputs are finite; a program needn't handle non-finite values.
Results may differ from a plain program's by a relative error of at most 0.0003.
Values sent between devices are 32-bit elements; how exact they have to be, the bound alone decides.
A program may use at most 128 MiB of HBM per device.

v0:
```python
import jax
import jax.numpy as jnp
from jax import lax
from jax.sharding import PartitionSpec as P

BITS = 6
LEVELS = 4


def paired(state, bit):
    count = state.shape[0]
    stride = 1 << bit
    shaped = state.reshape(count // (2 * stride), 2, stride, state.shape[1], state.shape[2])
    return shaped[:, ::-1].reshape(state.shape)


def contract(rows, state, other):
    stacked = jnp.concatenate([state, other], axis=1)
    return jnp.einsum(
        "brk,bke->bre",
        rows,
        stacked,
        precision=lax.Precision.HIGHEST,
        preferred_element_type=jnp.float32,
    )


def level_product(rows_dev, state, other):
    return contract(lax.all_gather(rows_dev, "exc", axis=1, tiled=True), state, other)


def regroup(state, groups):
    shaped = state.reshape(groups, state.shape[0] // groups, state.shape[1], state.shape[2])
    return lax.all_to_all(shaped, "space", split_axis=0, concat_axis=0, tiled=True).reshape(
        state.shape
    )


def restore(state, groups):
    shaped = state.reshape(groups, state.shape[0] // groups, state.shape[1], state.shape[2])
    return lax.all_to_all(shaped, "space", split_axis=0, concat_axis=0, tiled=True).reshape(
        state.shape
    )


def body(coeff, factors):
    blocks_dev = coeff.shape[0]
    local_bits = blocks_dev.bit_length() - 1
    groups = lax.axis_size("space")
    group_bits = groups.bit_length() - 1
    first_bit = BITS - LEVELS
    cross_start = min(LEVELS, max(0, local_bits - first_bit))
    level_rows = [factors[level] for level in range(LEVELS)]
    moved = factors[cross_start:]
    shaped = moved.reshape(
        moved.shape[0], groups, blocks_dev // groups, moved.shape[2], moved.shape[3]
    )
    shaped = lax.all_to_all(shaped, "space", split_axis=1, concat_axis=1, tiled=True).reshape(
        moved.shape
    )
    level_rows = level_rows[:cross_start] + [shaped[index] for index in range(LEVELS - cross_start)]
    state = coeff
    for level in range(LEVELS):
        bit = first_bit + level
        if bit < local_bits:
            other = paired(state, bit)
        else:
            if level == cross_start:
                state = regroup(state, groups)
            other = paired(state, bit - group_bits)
        state = level_product(level_rows[level], state, other)
    state = restore(state, groups)
    return state


def solution(mesh):
    return jax.shard_map(
        body,
        mesh=mesh,
        in_specs=(P("space", None, "exc"), P(None, "space", "exc", None)),
        out_specs=P("space", None, "exc"),
        check_vma=False,
    )
```

profile of v0, /device:TPU:1, one launch (start us, length us, event | category | flops | bytes accessed | tf_op | source)
XLA Modules:
  0.0 534.3 jit_solution(10234973929096856032)
XLA Ops:
  6.5 0.0 slice-start
  6.5 0.0 all-gather.11.cloned.1.call-start
  6.5 3.3 fusion.22
  9.8 0.0 all-gather.11.cloned.1.call-update
  9.9 0.0 all-gather.13.cloned.1.call-start
  9.9 0.7 all-gather.13.cloned.1.call-update
  10.6 0.0 all-gather.7.cloned.1.call-start
  10.7 0.0 slice-done
  10.7 0.2 copy.16
  10.9 28.3 %all_to_all.15 = f32[2,4,4,32,512]{4,3,2,0,1:T(8,128)S(1)} all-to-all(f32[2,4,4,32,512]{4,3,2,0,1:T(8,128)S(1)} %copy.16), channel_id=1, replica_groups=mesh['space'=4,'exc'=8] {'space'}, dimensions={1} | all-to-all | bytes 4194304 | tf_op jit(solution)/shard_map/all_to_all | solution.py:58
  39.2 1.6 fusion.23
  40.8 0.0 all-gather.7.cloned.1.call-update
  40.8 0.0 all-gather.9.cloned.1.call-start
  40.9 0.5 all-gather.9.cloned.1.call-update
  41.4 8.3 %rev.12 = f32[2,2,4,256,512]{4,3,2,1,0:T(8,128)} reverse(f32[2,2,4,256,512]{4,3,2,1,0:T(8,128)} %bitcast.36), dimensions={1} | reverse | bytes 16777216 | tf_op jit(solution)/shard_map/rev | solution.py:14
  49.7 44.9 %all-gather.11.cloned.1.call-done = f32[1,16,256,512]{3,2,1,0:T(8,128)} async-done(((f32[1,16,32,512]{3,2,1,0:T(8,128)}), f32[1,16,256,512]{3,2,1,0:T(8,128)}) %all-gather.11.cloned.1.call-update) | async-done | bytes 8388624 | tf_op jit(solution)/shard_map/all_gather | solution.py:29
  94.5 22.3 %fusion = f32[16,512,256]{1,2,0:T(8,128)} fusion(f32[16,256,512]{2,1,0:T(8,128)} %bitcast.41, f32[16,256,512]{2,1,0:T(8,128)} %param.2, f32[1,16,256,512]{3,2,1,0:T(8,128)} %all-gather.11.cloned.1.call-done), kind=kOutput, calls=%fused_computation | convolution fusion | flops 12889096192 | bytes 33554432 | tf_op jit(solution)/shard_map/brk,bke->bre/dot_general | solution.py:19
  116.8 8.2 %rev.13 = f32[1,2,8,256,512]{4,3,2,1,0:T(8,128)} reverse(f32[1,2,8,256,512]{4,3,2,1,0:T(8,128)} %bitcast.34), dimensions={1} | reverse | bytes 16777216 | tf_op jit(solution)/shard_map/rev | solution.py:14
  125.0 51.6 %all-gather.13.cloned.1.call-done = f32[1,16,256,512]{3,2,1,0:T(8,128)} async-done(((f32[1,16,32,512]{3,2,1,0:T(8,128)}), f32[1,16,256,512]{3,2,1,0:T(8,128)}) %all-gather.13.cloned.1.call-update) | async-done | bytes 8388624 | tf_op jit(solution)/shard_map/all_gather | solution.py:29
  176.7 50.1 %fusion.4 = f32[16,512,256]{2,1,0:T(8,128)} fusion(f32[16,256,512]{2,1,0:T(8,128)} %bitcast.39, f32[16,256,512]{2,1,0:T(8,128)} %bitcast.35, f32[1,16,256,512]{3,2,1,0:T(8,128)} %all-gather.13.cloned.1.call-done), kind=kOutput, calls=%fused_computation.4 | convolution fusion | flops 12889096192 | bytes 33554432 | tf_op jit(solution)/shard_map/brk,bke->bre/dot_general | solution.py:19
  226.8 99.8 %all_to_all.16 = f32[4,4,256,512]{2,3,1,0:T(8,128)} all-to-all(f32[4,4,256,512]{2,3,1,0:T(8,128)} %bitcast.42), channel_id=1, replica_groups=mesh['space'=4,'exc'=8] {'space'}, dimensions={0} | all-to-all | bytes 16777216 | tf_op jit(solution)/shard_map/all_to_all | solution.py:34
  326.6 9.9 %copy.15 = f32[2,2,4,256,512]{4,3,2,1,0:T(8,128)} copy(f32[2,2,4,256,512]{3,4,2,1,0:T(8,128)} %bitcast.31) | data formatting | bytes 16777216 | tf_op jit(solution)/shard_map/reshape;reshape | solution.py:13
  336.5 7.9 %rev.14 = f32[2,2,4,256,512]{4,3,2,1,0:T(8,128)} reverse(f32[2,2,4,256,512]{4,3,2,1,0:T(8,128)} %copy.15), dimensions={1} | reverse | bytes 16777216 | tf_op jit(solution)/shard_map/rev | solution.py:14
  344.4 9.9 %copy.14 = f32[4,4,256,512]{3,2,1,0:T(8,128)} copy(f32[4,4,256,512]{2,3,1,0:T(8,128)} %all_to_all.16) | data formatting | bytes 16777216 | tf_op jit(solution)/shard_map/all_to_all | solution.py:34
  354.3 0.0 all-gather.7.cloned.1.call-done
  354.3 21.6 %fusion.8 = f32[16,512,256]{1,2,0:T(8,128)} fusion(f32[16,256,512]{2,1,0:T(8,128)} %all-gather.7.cloned.1.call-done, f32[16,256,512]{2,1,0:T(8,128)} %bitcast.37, f32[16,256,512]{2,1,0:T(8,128)} %bitcast.38), kind=kOutput, calls=%fused_computation.8 | convolution fusion | flops 12889096192 | bytes 33554432 | tf_op jit(solution)/shard_map/brk,bke->bre/dot_general | solution.py:19
  375.9 8.1 %rev.15 = f32[1,2,8,256,512]{4,3,2,1,0:T(8,128)} reverse(f32[1,2,8,256,512]{4,3,2,1,0:T(8,128)} %bitcast.32), dimensions={1} | reverse | bytes 16777216 | tf_op jit(solution)/shard_map/rev | solution.py:14
  384.0 0.0 all-gather.9.cloned.1.call-done
  384.0 35.4 %fusion.12 = f32[16,512,256]{2,1,0:T(8,128)} fusion(f32[16,256,512]{2,1,0:T(8,128)} %all-gather.9.cloned.1.call-done, f32[16,256,512]{2,1,0:T(8,128)} %bitcast.40, f32[16,256,512]{2,1,0:T(8,128)} %bitcast.33), kind=kOutput, calls=%fused_computation.12 | convolution fusion | flops 12889096192 | bytes 33554432 | tf_op jit(solution)/shard_map/brk,bke->bre/dot_general | solution.py:19
  419.5 98.3 %all_to_all.17 = f32[4,4,256,512]{2,3,1,0:T(8,128)} all-to-all(f32[4,4,256,512]{2,3,1,0:T(8,128)} %bitcast.43), channel_id=1, replica_groups=mesh['space'=4,'exc'=8] {'space'}, dimensions={0} | all-to-all | bytes 16777216 | tf_op jit(solution)/shard_map/all_to_all | solution.py:41
  517.7 9.9 %copy.18 = f32[4,4,256,512]{3,2,1,0:T(8,128)} copy(f32[4,4,256,512]{2,3,1,0:T(8,128)} %all_to_all.17) | data formatting | bytes 16777216 | tf_op jit(solution)/shard_map/all_to_all | solution.py:41
Async XLA Ops:
  6.5 4.1 slice-start
  6.5 88.0 %all-gather.11.cloned.1.call-start = ((), (), s32[]{:S(2)}) async-start(), calls=%async_computation.5 | async-start | bytes 9437184 | tf_op jit(solution)/shard_map/all_gather | solution.py:29
  9.9 166.8 %all-gather.13.cloned.1.call-start = ((), (), s32[]{:S(2)}) async-start(), calls=%async_computation.6 | async-start | bytes 9437184 | tf_op jit(solution)/shard_map/all_gather | solution.py:29
  10.6 343.7 %all-gather.7.cloned.1.call-start = ((), (), s32[]{:S(2)}) async-start(), calls=%async_computation.3 | async-start | bytes 9437184 | tf_op jit(solution)/shard_map/all_gather | solution.py:29
  40.8 343.2 %all-gather.9.cloned.1.call-start = ((), (), s32[]{:S(2)}) async-start(), calls=%async_computation.4 | async-start | bytes 9437184 | tf_op jit(solution)/shard_map/all_gather | solution.py:29
Sparse Core Ops, SparseCore 0:
  10.0 84.4 all-gather.10
  96.1 80.5 all-gather.12
  178.3 80.5 all-gather.6
  260.3 80.5 all-gather.8
where the time goes:
time: 537 us; the launch traced here: 534 us
  blocking collectives  226 us (42%)
  matrix products  129 us (24%)
  waiting for transfers between devices  97.7 us (18%)
  local copies, waits for them, and re-layouts  67.2 us (13%)
  between operations  13.3 us (2%)
    dot_general x4, matrix products, contract(): jnp.einsum('brk,bke->bre', rows, stacked, precision=lax.Precision.HIGHEST...  129 us
    all_to_all x1, blocking collectives, regroup(): lax.all_to_all(shaped, 'space', split_axis=0, concat_axis=0, tiled=True)  99.8 us
    all_to_all x1, blocking collectives, restore(): lax.all_to_all(shaped, 'space', split_axis=0, concat_axis=0, tiled=True)  98.3 us
    all_gather x4, waiting for transfers between devices, level_product(): lax.all_gather(rows_dev, 'exc', axis=1, tiled=True)  96.5 us
    rev x4, local copies, waits for them, and re-layouts, paired(): return shaped[:, ::-1].reshape(state.shape)  32.5 us
    all_to_all x1, blocking collectives, body(): lax.all_to_all(shaped, 'space', split_axis=1, concat_axis=1, tiled=True)  28.3 us
  transfers between devices with their start and end apart: 4, of which 2 were waited for; matrix products, arithmetic and copies ran while one was open for 28% of the time, Pallas kernels for 0%

commit v1 on v0

v1 whole, which is shorter than its diff:
```python
import functools

import jax
import jax.numpy as jnp
from jax import lax
from jax.experimental import pallas as pl
from jax.experimental.pallas import tpu as pltpu
from jax.sharding import PartitionSpec as P

BITS = 6
LEVELS = 4
CORES = 2
AHEAD = 3
TILE = 256
PHASE = (0.0, 0.1, 4.5, 14.0)
UP, DOWN, SIDE = 0, 1, 2


def split(x):
    high = x.astype(jnp.bfloat16)
    low = (x - high.astype(jnp.float32)).astype(jnp.bfloat16)
    return high, low


def dot3(a, b):
    dot = functools.partial(jnp.dot, preferred_element_type=jnp.float32)
    return dot(a[0], b[0]) + (dot(a[0], b[1]) + dot(a[1], b[0]))


def kernel(local_levels, coeff, fac, out, full, other, state, load_sem, own_sem, recv_sem, send_sem, xsend, xrecv):
    space, exc = lax.axis_index("space"), lax.axis_index("exc")
    chips = lax.axis_size("exc") // CORES
    chip, core = exc // CORES, exc % CORES
    sibling = exc + 1 - 2 * core
    nloc, groups, rank, cols = state.shape
    rows = fac.shape[3]
    tile = min(TILE, cols)
    units = sorted(
        ((level, group) for level in range(LEVELS) for group in range(groups)),
        key=lambda u: 3 * u[1] + PHASE[u[0]],
    )

    def shard(unit, source):
        level, group = units[unit]
        start = pl.multiple_of(source * rows, rows)
        return full.at[level, :, group, pl.ds(start, rows), :]

    def mine(unit):
        level, group = units[unit]
        return fac.at[level, :, group]

    def own_copy(unit):
        return pltpu.make_async_copy(mine(unit), shard(unit, exc), own_sem.at[unit])

    def remote(unit, src_ref, source, way, target):
        return pltpu.make_async_remote_copy(
            src_ref=src_ref,
            dst_ref=shard(unit, source),
            send_sem=send_sem.at[unit, way, source // CORES],
            recv_sem=recv_sem.at[unit, source],
            device_id=(space, target),
            device_id_type=pl.DeviceIdType.MESH,
        )

    def arrive(unit, source):
        remote(unit, shard(unit, source), source, SIDE, sibling).wait_recv()

    def send_own(unit):
        @pl.when(chip < chips - 1)
        def _():
            remote(unit, mine(unit), exc, UP, exc + CORES).start()

        @pl.when(chip > 0)
        def _():
            remote(unit, mine(unit), exc, DOWN, exc - CORES).start()

        remote(unit, mine(unit), exc, SIDE, sibling).start()
        own_copy(unit).start()

    def relay(unit):
        def hop(distance, carry):
            @pl.when(chip >= distance)
            def _():
                source = exc - distance * CORES
                arrive(unit, source)

                @pl.when(chip < chips - 1)
                def _():
                    remote(unit, shard(unit, source), source, UP, exc + CORES).start()

                remote(unit, shard(unit, source), source, SIDE, sibling).start()

            @pl.when(chip + distance < chips)
            def _():
                source = exc + distance * CORES
                arrive(unit, source)

                @pl.when(chip > 0)
                def _():
                    remote(unit, shard(unit, source), source, DOWN, exc - CORES).start()

                remote(unit, shard(unit, source), source, SIDE, sibling).start()

            return carry

        lax.fori_loop(1, chips, hop, 0)

    def exchange(level, group):
        at = level - local_levels
        stride = 1 << at
        partner = space + stride - 2 * stride * ((space // stride) % 2)
        return pltpu.make_async_remote_copy(
            src_ref=state.at[:, group],
            dst_ref=other.at[at, :, group],
            send_sem=xsend.at[at, group],
            recv_sem=xrecv.at[at, group],
            device_id=(partner, exc),
            device_id_type=pl.DeviceIdType.MESH,
        )

    def load(group):
        return pltpu.make_async_copy(coeff.at[:, group], state.at[:, group], load_sem.at[group])

    def store(group):
        return pltpu.make_async_copy(state.at[:, group], out.at[:, group], load_sem.at[group])

    def product(level, group, block, own, partner):
        top = split(full[level, block, group, :, :rank])
        bottom = split(full[level, block, group, :, rank:])
        return dot3(top, own) + dot3(bottom, partner)

    def consume(unit):
        level, group = units[unit]
        own_copy(unit).wait()

        def landed(index, carry):
            arrive(unit, index * CORES + 1 - core)
            return carry

        lax.fori_loop(0, chips, landed, 0)
        if level == 0:
            load(group).wait()
        tiles = cols // tile
        if level < local_levels:
            stride = 1 << level

            def pair(step, carry):
                index = step // tiles
                low = index // stride * 2 * stride + index % stride
                high = low + stride
                at = pl.ds(pl.multiple_of(step % tiles * tile, tile), tile)
                first = split(state[low, group, :, at])
                second = split(state[high, group, :, at])
                state[low, group, :, at] = product(level, group, low, first, second)
                state[high, group, :, at] = product(level, group, high, second, first)
                return carry

            lax.fori_loop(0, nloc // 2 * tiles, pair, 0)
        else:
            exchange(level, group).wait()

            def single(step, carry):
                block = step // tiles
                at = pl.ds(pl.multiple_of(step % tiles * tile, tile), tile)
                first = split(state[block, group, :, at])
                second = split(other[level - local_levels, block, group, :, at])
                state[block, group, :, at] = product(level, group, block, first, second)
                return carry

            lax.fori_loop(0, nloc * tiles, single, 0)
        if level + 1 == LEVELS:
            store(group).start()
        elif level + 1 >= local_levels:
            exchange(level + 1, group).start()

    for group in range(groups):
        load(group).start()
    for unit in range(min(AHEAD, len(units))):
        send_own(unit)
    if local_levels == 0:
        for group in range(groups):
            load(group).wait()
            exchange(0, group).start()
    held = []
    for unit in range(len(units)):
        if unit + AHEAD < len(units):
            send_own(unit + AHEAD)
        relay(unit)
        for late in held:
            consume(late)
        held = []
        if units[unit] == (LEVELS - 2, groups - 1):
            held = [unit]
        else:
            consume(unit)

    for group in range(groups):
        store(group).wait()
    for unit in range(len(units)):

        def drained(index, carry):
            source = index * CORES + core
            done = functools.partial(remote, unit, shard(unit, source), source)

            @pl.when((index <= chip) & (chip < chips - 1))
            def _():
                done(UP, sibling).wait_send()

            @pl.when((index >= chip) & (chip > 0))
            def _():
                done(DOWN, sibling).wait_send()

            done(SIDE, sibling).wait_send()
            return carry

        lax.fori_loop(0, chips, drained, 0)


def body(coeff, factors):
    blocks, rank, cols = coeff.shape
    rows, width = factors.shape[2:]
    groups = 1 << (BITS - LEVELS)
    nloc = blocks // groups
    local_levels = nloc.bit_length() - 1
    devices = lax.axis_size("exc")
    units = LEVELS * groups
    crossing = LEVELS - local_levels
    dma = pltpu.SemaphoreType.DMA
    result = pl.pallas_call(
        functools.partial(kernel, local_levels),
        out_shape=jax.ShapeDtypeStruct((nloc, groups, rank, cols), jnp.float32),
        in_specs=[pl.BlockSpec(memory_space=pl.ANY)] * 2,
        out_specs=pl.BlockSpec(memory_space=pl.ANY),
        scratch_shapes=[
            pltpu.VMEM((LEVELS, nloc, groups, rank, width), jnp.float32),
            pltpu.VMEM((crossing, nloc, groups, rank, cols), jnp.float32),
            pltpu.VMEM((nloc, groups, rank, cols), jnp.float32),
            dma((groups,)),
            dma((units,)),
            dma((units, devices)),
            dma((units, 3, devices // CORES)),
            dma((crossing, groups)),
            dma((crossing, groups)),
        ],
        compiler_params=pltpu.CompilerParams(has_side_effects=True, vmem_limit_bytes=63 << 20),
    )(
        coeff.reshape(nloc, groups, rank, cols),
        factors.reshape(LEVELS, nloc, groups, rows, width),
    )
    return result.reshape(coeff.shape)


def solution(mesh):
    return jax.shard_map(
        body,
        mesh=mesh,
        in_specs=(P("space", None, "exc"), P(None, "space", "exc", None)),
        out_specs=P("space", None, "exc"),
        check_vma=False,
    )
```

time: 537 us -> 332 us (0.62)
  Pallas kernels: 0 us -> 324 us
  blocking collectives: 226 us -> 0 us
  matrix products: 129 us -> 0 us
  waiting for transfers between devices: 97.7 us -> 0 us
  local copies, waits for them, and re-layouts: 67.2 us -> 8.12 us
  between operations: 13.3 us -> 0.01 us
    pallas_call x0 -> x1, Pallas kernels: none -> 324 us  [body(): pl.pallas_call(functools.partial(kernel, local_levels), out_shape=jax.Sha...]
    all_to_all x3 -> x0, blocking collectives: 226 us -> none  [the longest x1 99.8 us: regroup(): lax.all_to_all(shaped, 'space', split_axis=0, concat_axis=0, tiled=True)]
    dot_general x4 -> x0, matrix products: 129 us -> none  [contract(): jnp.einsum('brk,bke->bre', rows, stacked, precision=lax.Precision.HIGHEST...]
    all_gather x4 -> x0, waiting for transfers between devices: 96.5 us -> none  [level_product(): lax.all_gather(rows_dev, 'exc', axis=1, tiled=True)]
    rev x4 -> x0, local copies, waits for them, and re-layouts: 32.5 us -> none  [paired(): return shaped[:, ::-1].reshape(state.shape)]
    all_to_all x2 -> x0, local copies, waits for them, and re-layouts: 19.7 us -> none  [the longest x1 9.87 us: restore(): lax.all_to_all(shaped, 'space', split_axis=0, concat_axis=0, tiled=True)]
    another operation x1 -> x0, local copies, waits for them, and re-layouts: 9.89 us -> none  [paired(): state.reshape(count // (2 * stride), 2, stride, state.shape[1], state.sha...]
    unnamed x0 -> x1, local copies, waits for them, and re-layouts: none -> 8.12 us
  transfers between devices with their start and end apart: 4 -> 0, of which waited for: 2 -> 0; matrix products, arithmetic and copies ran while one was open for 28% -> 0% of each run, Pallas kernels for 0% -> 0%
where the time goes in v1:
time: 332 us
  Pallas kernels  324 us (98%)
  local copies, waits for them, and re-layouts  8.12 us (2%)
    pallas_call x1, Pallas kernels, body(): pl.pallas_call(functools.partial(kernel, local_levels), out_shape=jax.Sha...  324 us
    unnamed x1, local copies, waits for them, and re-layouts  8.12 us

profile of v1, /device:TPU:1, one launch (start us, length us, event | category | flops | bytes accessed | tf_op | source)
XLA Modules:
  0.0 332.2 jit_solution(10873028165497895058)
XLA Ops:
  0.0 324.1 %shard_map.28 = f32[4,4,256,512]{3,2,1,0:T(8,128)} custom-call(f32[4,4,256,512]{3,2,1,0:T(8,128)} %bitcast.4, f32[4,4,4,32,512]{4,3,2,1,0:T(8,128)} %bitcast.5), custom_call_target="tpu_custom_call" | custom-call | tf_op jit(solution)/shard_map/pallas_call | solution.py:229
  324.1 8.1 %copy.4 = f32[16,256,512]{2,1,0:T(8,128)} copy(f32[16,256,512]{2,1,0:T(8,128)} %bitcast.3) | data formatting | bytes 16777216

commit v2 on v1

--- a/solution.py
+++ b/solution.py
@@ -10,9 +10,10 @@
 BITS = 6
 LEVELS = 4
 CORES = 2
-AHEAD = 3
+AHEAD = 2
 TILE = 256
 PHASE = (0.0, 0.1, 4.5, 14.0)
+LAG = (0, 0, 0, 0)
 UP, DOWN, SIDE = 0, 1, 2
 
 
@@ -27,7 +28,7 @@
     return dot(a[0], b[0]) + (dot(a[0], b[1]) + dot(a[1], b[0]))
 
 
-def kernel(local_levels, coeff, fac, out, full, other, state, load_sem, own_sem, recv_sem, send_sem, xsend, xrecv):
+def kernel(local_levels, coeff, fac, out, full, other, state, load_sem, store_sem, own_sem, recv_sem, send_sem, xsend, xrecv):
     space, exc = lax.axis_index("space"), lax.axis_index("exc")
     chips = lax.axis_size("exc") // CORES
     chip, core = exc // CORES, exc % CORES
@@ -105,15 +106,15 @@
 
         lax.fori_loop(1, chips, hop, 0)
 
-    def exchange(level, group):
+    def exchange(level, group, block):
         at = level - local_levels
         stride = 1 << at
         partner = space + stride - 2 * stride * ((space // stride) % 2)
         return pltpu.make_async_remote_copy(
-            src_ref=state.at[:, group],
-            dst_ref=other.at[at, :, group],
-            send_sem=xsend.at[at, group],
-            recv_sem=xrecv.at[at, group],
+            src_ref=state.at[block, group],
+            dst_ref=other.at[at, block, group],
+            send_sem=xsend.at[at, group, block],
+            recv_sem=xrecv.at[at, group, block],
             device_id=(partner, exc),
             device_id_type=pl.DeviceIdType.MESH,
         )
@@ -121,8 +122,16 @@
     def load(group):
         return pltpu.make_async_copy(coeff.at[:, group], state.at[:, group], load_sem.at[group])
 
-    def store(group):
-        return pltpu.make_async_copy(state.at[:, group], out.at[:, group], load_sem.at[group])
+    def store(group, block):
+        return pltpu.make_async_copy(
+            state.at[block, group], out.at[block, group], store_sem.at[group, block]
+        )
+
+    def pass_on(level, group, block):
+        if level + 1 == LEVELS:
+            store(group, block).start()
+        elif level + 1 >= local_levels:
+            exchange(level + 1, group, block).start()
 
     def product(level, group, block, own, partner):
         top = split(full[level, block, group, :, :rank])
@@ -144,34 +153,43 @@
         if level < local_levels:
             stride = 1 << level
 
-            def pair(step, carry):
-                index = step // tiles
+            def pair(index, carry):
                 low = index // stride * 2 * stride + index % stride
                 high = low + stride
-                at = pl.ds(pl.multiple_of(step % tiles * tile, tile), tile)
-                first = split(state[low, group, :, at])
-                second = split(state[high, group, :, at])
-                state[low, group, :, at] = product(level, group, low, first, second)
-                state[high, group, :, at] = product(level, group, high, second, first)
+
+                def part(step, inner):
+                    at = pl.ds(pl.multiple_of(step * tile, tile), tile)
+                    first = split(state[low, group, :, at])
+                    second = split(state[high, group, :, at])
+                    state[low, group, :, at] = product(level, group, low, first, second)
+                    state[high, group, :, at] = product(level, group, high, second, first)
+                    return inner
+
+                lax.fori_loop(0, tiles, part, 0)
+                pass_on(level, group, low)
+                pass_on(level, group, high)
                 return carry
 
-            lax.fori_loop(0, nloc // 2 * tiles, pair, 0)
+            lax.fori_loop(0, nloc // 2, pair, 0)
         else:
-            exchange(level, group).wait()
+            half = max(nloc // 2, 1)
 
             def single(step, carry):
-                block = step // tiles
-                at = pl.ds(pl.multiple_of(step % tiles * tile, tile), tile)
-                first = split(state[block, group, :, at])
-                second = split(other[level - local_levels, block, group, :, at])
-                state[block, group, :, at] = product(level, group, block, first, second)
+                block = step % 2 * half + step // 2
+                exchange(level, group, block).wait()
+
+                def part(step, inner):
+                    at = pl.ds(pl.multiple_of(step * tile, tile), tile)
+                    first = split(state[block, group, :, at])
+                    second = split(other[level - local_levels, block, group, :, at])
+                    state[block, group, :, at] = product(level, group, block, first, second)
+                    return inner
+
+                lax.fori_loop(0, tiles, part, 0)
+                pass_on(level, group, block)
                 return carry
 
-            lax.fori_loop(0, nloc * tiles, single, 0)
-        if level + 1 == LEVELS:
-            store(group).start()
-        elif level + 1 >= local_levels:
-            exchange(level + 1, group).start()
+            lax.fori_loop(0, nloc, single, 0)
 
     for group in range(groups):
         load(group).start()
@@ -180,22 +198,21 @@
     if local_levels == 0:
         for group in range(groups):
             load(group).wait()
-            exchange(0, group).start()
-    held = []
+            for block in range(nloc):
+                exchange(0, group, block).start()
+    due = sorted((unit + LAG[units[unit][0]], unit) for unit in range(len(units)))
     for unit in range(len(units)):
+        relay(unit)
         if unit + AHEAD < len(units):
             send_own(unit + AHEAD)
-        relay(unit)
-        for late in held:
-            consume(late)
-        held = []
-        if units[unit] == (LEVELS - 2, groups - 1):
-            held = [unit]
-        else:
-            consume(unit)
+        while due and due[0][0] <= unit:
+            consume(due.pop(0)[1])
+    while due:
+        consume(due.pop(0)[1])
 
     for group in range(groups):
-        store(group).wait()
+        for block in range(nloc):
+            store(group, block).wait()
     for unit in range(len(units)):
 
         def drained(index, carry):
@@ -236,11 +253,12 @@
             pltpu.VMEM((crossing, nloc, groups, rank, cols), jnp.float32),
             pltpu.VMEM((nloc, groups, rank, cols), jnp.float32),
             dma((groups,)),
+            dma((groups, nloc)),
             dma((units,)),
             dma((units, devices)),
             dma((units, 3, devices // CORES)),
-            dma((crossing, groups)),
-            dma((crossing, groups)),
+            dma((crossing, groups, nloc)),
+            dma((crossing, groups, nloc)),
         ],
         compiler_params=pltpu.CompilerParams(has_side_effects=True, vmem_limit_bytes=63 << 20),
     )(

time: 332 us -> 312 us (0.940)
  Pallas kernels: 324 us -> 304 us
    pallas_call x1, Pallas kernels: 324 us -> 304 us  [body(): pl.pallas_call(functools.partial(kernel, local_levels), out_shape=jax.Sha...]
where the time goes in v2:
time: 312 us
  Pallas kernels  304 us (97%)
  local copies, waits for them, and re-layouts  8.12 us (3%)
    pallas_call x1, Pallas kernels, body(): pl.pallas_call(functools.partial(kernel, local_levels), out_shape=jax.Sha...  304 us
    unnamed x1, local copies, waits for them, and re-layouts  8.12 us

profile of v2, /device:TPU:1, one launch (start us, length us, event | category | flops | bytes accessed | tf_op | source)
XLA Modules:
  0.0 311.8 jit_solution(4790277636868477828)
XLA Ops:
  0.0 303.7 %shard_map.28 = f32[4,4,256,512]{3,2,1,0:T(8,128)} custom-call(f32[4,4,256,512]{3,2,1,0:T(8,128)} %bitcast.4, f32[4,4,4,32,512]{4,3,2,1,0:T(8,128)} %bitcast.5), custom_call_target="tpu_custom_call" | custom-call | tf_op jit(solution)/shard_map/pallas_call | solution.py:246
  303.7 8.1 %copy.4 = f32[16,256,512]{2,1,0:T(8,128)} copy(f32[16,256,512]{2,1,0:T(8,128)} %bitcast.3) | data formatting | bytes 16777216
